TPU v7x, 128 devices: a whole 4x4x4 slice. The times are simulated.
128 devices in a mesh: dp: 32 (over x, z, core), tensor: 4 (over y).
Axes of the slice: x: 4, y: 4, z: 4, core: 2. Of those that a mesh axis runs over, the one named last changes fastest.
Arguments:
- hidden_in: bfloat16 [32768, 768], P('dp'), may hold values from -6 to 6
- segments: int32 [32768], P('dp'), may hold values from 0 to 63, as said below
- positions: int32 [32768], P('dp'), may hold values from 0 to 1023, as said below
- first_gain: float32 [768], replicated, may hold values from 0.1 to 1.9
- first_shift: float32 [768], replicated, may hold values from -2 to 2
- heads_weight: bfloat16 [768, 2304], P(None, 'tensor'), may hold values from -0.21875 to 0.21875
- heads_bias: float32 [2304], P('tensor'), may hold values from -2 to 2
- dense_weight: bfloat16 [768, 768], P('tensor'), may hold values from -0.875 to 0.875
- dense_bias: float32 [768], replicated, may hold values from -3 to 3
- second_gain: float32 [768], replicated, may hold values from 0.1 to 1.9
- second_shift: float32 [768], replicated, may hold values from -2 to 2
- expand_weight: bfloat16 [768, 3072], P(None, 'tensor'), may hold values from -0.21875 to 0.21875
- expand_bias: float32 [3072], P('tensor'), may hold values from -3 to 3
- shrink_weight: bfloat16 [3072, 768], P('tensor'), may hold values from -0.109375 to 0.109375
- shrink_bias: float32 [768], replicated, may hold values from -3 to 3
- cotangent: bfloat16 [32768, 768], P('dp'), may hold values from -6 to 6
Outputs:
- hidden_out: bfloat16 [32768, 768], P('dp')
- hidden_gradient: bfloat16 [32768, 768], P('dp')
- first_gain_gradient: float32 [768], replicated
- first_shift_gradient: float32 [768], replicated
- heads_weight_gradient: float32 [768, 2304], P(None, 'tensor')
- heads_bias_gradient: float32 [2304], P('tensor')
- dense_weight_gradient: float32 [768, 768], P('tensor')
- dense_bias_gradient: float32 [768], replicated
- second_gain_gradient: float32 [768], replicated
- second_shift_gradient: float32 [768], replicated
- expand_weight_gradient: float32 [768, 3072], P(None, 'tensor')
- expand_bias_gradient: float32 [3072], P('tensor')
- shrink_weight_gradient: float32 [3072, 768], P('tensor')
- shrink_bias_gradient: float32 [768], replicated
Inputs may be any that keep to these rules, and one draw needn't show every extreme that they name: `segments`: each sequence s of 1024 tokens (rows s * 1024 to s * 1024 + 1023) holds 2 documents numbered s * 2 to s * 2 + 1 in order, segment numbers never falling; each document has 1024 // 2 - 2 * (128) tokens or more. Within a document positions rise by one from token to token; the first document of each sequence starts at 0; the last document of the first sequence ends at the largest position.
All inputs are finite; a program needn't handle non-finite values.
Results may differ from a plain program's by a relative error of at most 0.012.
The roundings to bfloat16 on the way count: a program that leaves them out, or rounds other values in their place, can miss the bound.
Values sent between devices are 32-bit elements; how exact they have to be, the bound alone decides.
No kernel may reach another device: no remote copies, remote signals or barrier semaphores. Data moves between devices by JAX's collectives and lax.ppermute only.
A program may use at most 128 MiB of HBM per device.

v0:
```python
import math
import jax
import jax.numpy as jnp
from jax import lax
from jax.sharding import PartitionSpec as P

HD = 64
ROT = 16
epsilon = 1e-05
rotary_base = 10000.0
block_limit = 512


def contract(pattern, left_op, right_op):
    return jnp.einsum(pattern, left_op, right_op, preferred_element_type=jnp.float32)


def layer_norm(wide_input):
    center = wide_input - jnp.mean(wide_input, axis=-1, keepdims=True)
    norm_scale = lax.rsqrt(jnp.mean(center * center, axis=-1, keepdims=True) + epsilon)
    return (center * norm_scale, norm_scale)


def norm_backward(upstream, normed, norm_scale, gain_row):
    scaled = upstream * gain_row
    return norm_scale * (
        scaled
        - jnp.mean(scaled, axis=-1, keepdims=True)
        - normed * jnp.mean(scaled * normed, axis=-1, keepdims=True)
    )


def gelu_value(hidden_pre):
    return hidden_pre * 0.5 * (1.0 + lax.erf(hidden_pre * (1.0 / math.sqrt(2.0))))


def gelu_slope(hidden_pre):
    return 0.5 * (1.0 + lax.erf(hidden_pre * (1.0 / math.sqrt(2.0)))) + hidden_pre * jnp.exp(
        -0.5 * hidden_pre * hidden_pre
    ) * (1.0 / math.sqrt(2.0 * math.pi))


def rotary_tables(seq_positions):
    half_rot = ROT // 2
    frequency = rotary_base ** (jnp.arange(half_rot).astype(jnp.float32) * (-2.0 / ROT))
    angles = seq_positions.astype(jnp.float32)[:, None] * frequency[None, :]
    angles = jnp.concatenate([angles, angles], axis=1)
    return (jnp.cos(angles), jnp.sin(angles))


def half_turn(front_dims):
    half_rot = ROT // 2
    return jnp.concatenate([-front_dims[..., half_rot:], front_dims[..., :half_rot]], axis=-1)


def rotate_forward(vectors, cosine, sine_table):
    front_dims = vectors[..., :ROT]
    turned = front_dims * cosine[:, None, :] + half_turn(front_dims) * sine_table[:, None, :]
    return jnp.concatenate([turned, vectors[..., ROT:]], axis=-1)


def rotate_backward(upstream, cosine, sine_table):
    front_dims = upstream[..., :ROT]
    turned = front_dims * cosine[:, None, :] - half_turn(front_dims * sine_table[:, None, :])
    return jnp.concatenate([turned, upstream[..., ROT:]], axis=-1)


def mask_block(seq_segments, first_row, last_row):
    token_index = jnp.arange(last_row)
    causal_ok = token_index[first_row:last_row, None] >= token_index[None, :]
    same_doc = seq_segments[first_row:last_row, None] == seq_segments[None, :last_row]
    return causal_ok & same_doc


def block_scores(queries, key_rows, seq_segments, first_row, last_row):
    scores = contract("hqd,hkd->hqk", queries[:, first_row:last_row], key_rows[:, :last_row]) * (
        1.0 / math.sqrt(HD)
    )
    return jnp.where(mask_block(seq_segments, first_row, last_row)[None], scores, -1e30)


def attend_forward(queries, key_rows, value_rows, seq_segments):
    row_count = queries.shape[1]
    block_size = min(row_count, block_limit)
    context_parts = []
    logsum_parts = []
    for first_row in range(0, row_count, block_size):
        last_row = first_row + block_size
        scores = block_scores(queries, key_rows, seq_segments, first_row, last_row)
        row_max = jnp.max(scores, axis=-1, keepdims=True)
        weights = jnp.exp(scores - row_max)
        row_total = jnp.sum(weights, axis=-1, keepdims=True)
        weights_low = (weights / row_total).astype(jnp.bfloat16)
        context_parts.append(
            contract("hqk,hkd->hqd", weights_low, value_rows[:, :last_row]).astype(jnp.bfloat16)
        )
        logsum_parts.append((row_max + jnp.log(row_total))[..., 0])
    return (jnp.concatenate(context_parts, axis=1), jnp.concatenate(logsum_parts, axis=1))


def attend_backward(queries, key_rows, value_rows, contexts, logsum, context_grad, seq_segments):
    row_count = queries.shape[1]
    block_size = min(row_count, block_limit)
    query_parts = []
    key_grad = jnp.zeros(key_rows.shape, jnp.float32)
    value_grad = jnp.zeros(value_rows.shape, jnp.float32)
    for first_row in range(0, row_count, block_size):
        last_row = first_row + block_size
        scores = block_scores(queries, key_rows, seq_segments, first_row, last_row)
        probs_back = jnp.exp(scores - logsum[:, first_row:last_row, None])
        probs_low = probs_back.astype(jnp.bfloat16)
        grad_block = context_grad[:, first_row:last_row]
        value_grad = value_grad.at[:, :last_row].add(
            contract("hqk,hqd->hkd", probs_low, grad_block)
        )
        prob_grad = contract("hqd,hkd->hqk", grad_block, value_rows[:, :last_row])
        row_inner = jnp.sum(
            grad_block.astype(jnp.float32) * contexts[:, first_row:last_row].astype(jnp.float32),
            axis=-1,
            keepdims=True,
        )
        score_grad = (probs_back * (prob_grad - row_inner) * (1.0 / math.sqrt(HD))).astype(
            jnp.bfloat16
        )
        query_parts.append(contract("hqk,hkd->hqd", score_grad, key_rows[:, :last_row]))
        key_grad = key_grad.at[:, :last_row].add(
            contract("hqk,hqd->hkd", score_grad, queries[:, first_row:last_row])
        )
    return (jnp.concatenate(query_parts, axis=1), key_grad, value_grad)


def on_device(
    hidden_in,
    segments,
    positions,
    first_gain,
    first_shift,
    heads_weight,
    heads_bias,
    dense_weight,
    dense_bias,
    second_gain,
    second_shift,
    expand_weight,
    expand_bias,
    shrink_weight,
    shrink_bias,
    cotangent,
):
    row_count = hidden_in.shape[0]
    head_count = heads_weight.shape[1] // (3 * HD)
    wide_input = hidden_in.astype(jnp.float32)
    normed, norm_scale = layer_norm(wide_input)
    first_input = (normed * first_gain + first_shift).astype(jnp.bfloat16)
    second_input = (normed * second_gain + second_shift).astype(jnp.bfloat16)
    mixed_rows = (
        jnp.dot(first_input, heads_weight, preferred_element_type=jnp.float32) + heads_bias
    ).reshape(row_count, head_count, 3, HD)
    cosine, sine_table = rotary_tables(positions)
    queries = (
        rotate_forward(mixed_rows[:, :, 0], cosine, sine_table)
        .astype(jnp.bfloat16)
        .transpose(1, 0, 2)
    )
    key_rows = (
        rotate_forward(mixed_rows[:, :, 1], cosine, sine_table)
        .astype(jnp.bfloat16)
        .transpose(1, 0, 2)
    )
    value_rows = mixed_rows[:, :, 2].astype(jnp.bfloat16).transpose(1, 0, 2)
    contexts, logsum = attend_forward(queries, key_rows, value_rows, segments)
    context_rows = contexts.transpose(1, 0, 2).reshape(row_count, head_count * HD)
    hidden_pre = (
        jnp.dot(second_input, expand_weight, preferred_element_type=jnp.float32) + expand_bias
    )
    activated = gelu_value(hidden_pre).astype(jnp.bfloat16)
    branch_part = jnp.dot(context_rows, dense_weight, preferred_element_type=jnp.float32) + jnp.dot(
        activated, shrink_weight, preferred_element_type=jnp.float32
    )
    branch = lax.psum(branch_part, "tensor")
    hidden_out = (wide_input + branch + dense_bias + shrink_bias).astype(jnp.bfloat16)
    grad_rows = cotangent.astype(jnp.float32)
    out_bias_grad = jnp.sum(grad_rows, axis=0)
    shrink_grad = jnp.dot(activated.T, cotangent, preferred_element_type=jnp.float32)
    pre_grad = jnp.dot(cotangent, shrink_weight.T, preferred_element_type=jnp.float32) * gelu_slope(
        hidden_pre
    )
    expand_bias_grad = jnp.sum(pre_grad, axis=0)
    pre_low = pre_grad.astype(jnp.bfloat16)
    expand_grad = jnp.dot(second_input.T, pre_low, preferred_element_type=jnp.float32)
    dense_grad = jnp.dot(context_rows.T, cotangent, preferred_element_type=jnp.float32)
    context_grad = jnp.dot(cotangent, dense_weight.T, preferred_element_type=jnp.float32).astype(
        jnp.bfloat16
    )
    context_grad = context_grad.reshape(row_count, head_count, HD).transpose(1, 0, 2)
    query_grad, key_grad, value_grad = attend_backward(
        queries, key_rows, value_rows, contexts, logsum, context_grad, segments
    )
    query_grad = rotate_backward(query_grad.transpose(1, 0, 2), cosine, sine_table)
    key_grad = rotate_backward(key_grad.transpose(1, 0, 2), cosine, sine_table)
    mixed_grad = jnp.stack([query_grad, key_grad, value_grad.transpose(1, 0, 2)], axis=2).reshape(
        row_count, head_count * 3 * HD
    )
    heads_bias_grad = jnp.sum(mixed_grad, axis=0)
    mixed_low = mixed_grad.astype(jnp.bfloat16)
    heads_grad = jnp.dot(first_input.T, mixed_low, preferred_element_type=jnp.float32)
    first_up = jnp.dot(mixed_low, heads_weight.T, preferred_element_type=jnp.float32)
    second_up = jnp.dot(pre_low, expand_weight.T, preferred_element_type=jnp.float32)
    input_part = norm_backward(first_up, normed, norm_scale, first_gain) + norm_backward(
        second_up, normed, norm_scale, second_gain
    )
    norm_terms = jnp.stack(
        [
            jnp.sum(first_up * normed, axis=0),
            jnp.sum(first_up, axis=0),
            jnp.sum(second_up * normed, axis=0),
            jnp.sum(second_up, axis=0),
        ]
    )
    norm_terms = lax.psum(norm_terms, ("dp", "tensor"))
    summed_input = lax.psum(input_part, "tensor")
    hidden_gradient = (grad_rows + summed_input).astype(jnp.bfloat16)
    (
        heads_grad,
        heads_bias_grad,
        dense_grad,
        out_bias_grad,
        expand_grad,
        expand_bias_grad,
        shrink_grad,
    ) = lax.psum(
        (
            heads_grad,
            heads_bias_grad,
            dense_grad,
            out_bias_grad,
            expand_grad,
            expand_bias_grad,
            shrink_grad,
        ),
        "dp",
    )
    return (
        hidden_out,
        hidden_gradient,
        norm_terms[0],
        norm_terms[1],
        heads_grad,
        heads_bias_grad,
        dense_grad,
        out_bias_grad,
        norm_terms[2],
        norm_terms[3],
        expand_grad,
        expand_bias_grad,
        shrink_grad,
        out_bias_grad,
    )


def solution(mesh):
    placed = (
        P("dp", None),
        P("dp"),
        P("dp"),
        P(),
        P(),
        P(None, "tensor"),
        P("tensor"),
        P("tensor", None),
        P(),
        P(),
        P(),
        P(None, "tensor"),
        P("tensor"),
        P("tensor", None),
        P(),
        P("dp", None),
    )
    return jax.shard_map(
        on_device,
        mesh=mesh,
        in_specs=placed,
        out_specs=(
            P("dp", None),
            P("dp", None),
            P(),
            P(),
            P(None, "tensor"),
            P("tensor"),
            P("tensor", None),
            P(),
            P(),
            P(),
            P(None, "tensor"),
            P("tensor"),
            P("tensor", None),
            P(),
        ),
        check_vma=False,
    )
```

profile of v0, /device:TPU:0, one launch (start us, length us, event | category | flops | bytes accessed | tf_op | source)
XLA Modules:
  0.0 334.0 jit_solution(16505256504611670689)
XLA Ops:
  7.3 1.8 convert_reduce_fusion
  9.1 2.0 fusion.25
  15.7 2.0 fusion
  17.7 2.1 fusion.56
  24.8 3.0 multiply_convert_fusion
  30.4 1.9 fusion.52
  34.2 1.9 multiply_convert_fusion.2
  36.2 3.4 %fusion.98 = (f32[768]{0:T(1024)}, bf16[1024,768]{1,0:T(8,128)(2,1)S(1)}) fusion(f32[1024,768]{1,0:T(8,128)S(1)} %get-tuple-element.128, f32[768]{0:T(1024)S(1)} %copy-done.27, bf16[1024,768]{1,0:T(8,128)(2,1)S(1)} %copy-done.3, bf16[768,768]{1,0:T(8,128)(2,1)S(1)} %copy-done.24), kind=kOutput, calls=%fused_computation.156 | convolution fusion | flops 1217395968 | bytes 7477248 | tf_op jit(solution)/shard_map/dot_general | solution.py:185
  39.6 1.4 fusion.60
  41.1 3.7 %fusion.23 = (f32[768]{0:T(1024)}, f32[1024]{0:T(1024)S(1)}, f32[1024]{0:T(1024)S(1)}, f32[768]{0:T(1024)}, f32[768]{0:T(1024)}, /*index=5*/f32[1024]{0:T(1024)S...) fusion(bf16[1024,768]{1,0:T(8,128)(2,1)S(1)} %copy-done.1, f32[1024]{0:T(1024)S(1)} %add_rsqrt_fusion, ...), kind=kOutput, calls=%fused_computation.34 | convolution fusion | flops 919331840 | bytes 9971712 | tf_op jit(solution)/shard_map/dot_general | solution.py:207
  46.3 2.3 convolution_add_fusion
  48.6 3.0 fusion.20
  51.7 2.8 fusion.102
  54.6 4.8 %fusion.103 = f32[768,768]{1,0:T(8,128)} fusion(bf16[1024,768]{1,0:T(8,128)(2,1)} %copy-done.32, bf16[1024,768]{1,0:T(8,128)(2,1)} %param.43), kind=kOutput, calls=%fused_computation.159 | convolution fusion | flops 1207959552 | bytes 5505024 | tf_op jit(solution)/shard_map/dot_general | solution.py:184
  59.4 2.6 fusion.92
  62.0 3.2 fusion.58
  65.2 1.6 fusion.42
  67.0 71.8 %psum.72 = f32[4,768]{1,0:T(4,128)S(1)} all-reduce(f32[4,768]{1,0:T(4,128)S(1)} %pad_maximum_fusion.3), channel_id=1, replica_groups=mesh['dp'=32,'tensor'=4] {'dp','tensor'}, use_global_device_ids=true, to_apply=%region_18.19 | all-reduce | flops 3072 | bytes 24576 | tf_op jit(solution)/shard_map/psum | solution.py:220
  139.4 43.5 %all-reduce.10.cloned.1.call-done = (f32[1024,768]{1,0:T(8,128)}, f32[1024,768]{1,0:T(8,128)}) async-done(((f32[1024,768]{1,0:T(8,128)}, f32[1024,768]{1,0:T(8,128)}), (f32[1024,768]{1,0:T(8,128)}, f32[1024,768]{1,0:T(8,128)})) %all-reduce.10.cloned.1.call-update) | async-done | bytes 6291472 | tf_op jit(solution)/shard_map/psum | solution.py:180
  182.9 4.2 %convert_reduce_fusion.1 = (f32[768]{0:T(1024)S(1)}, bf16[1024,768]{1,0:T(8,128)(2,1)}) fusion(bf16[1024,768]{1,0:T(8,128)(2,1)} %param.43, f32[1024,768]{1,0:T(8,128)} %get-tuple-element.104), kind=kLoop, calls=%fused_computation.11 | loop fusion | flops 3144960 | bytes 6294528 | tf_op jit(solution)/shard_map/reduce_sum | solution.py:183
  187.1 129.2 %all-reduce.2 = (f32[576]{0:T(1024)}, f32[768]{0:T(1024)S(1)}, f32[768]{0:T(1024)}) all-reduce(f32[576]{0:T(1024)S(1)} %reduce_sum.170, f32[768]{0:T(1024)S(1)} %get-tuple-element.107, f32[768]{0:T(1024)S(1)} %copy-done.17), channel_id=1, replica_groups=mesh['dp'=32,'tensor'=4] {'dp'}, use_global_device_ids=true, to_apply=%region_21.22 | all-reduce | flops 2112 | bytes 16896 | tf_op jit(solution)/shard_map/psum | solution.py:231
  316.3 3.5 %fusion.29 = bf16[1024,768]{1,0:T(8,128)(2,1)} fusion(f32[1024,768]{1,0:T(8,128)} %get-tuple-element.103, bf16[1024,768]{1,0:T(8,128)(2,1)S(1)} %copy-done.1, f32[768]{0:T(1024)S(1)} %copy-done.15, f32[768]{0:T(1024)S(1)} %copy-done.16), kind=kLoop, calls=%fused_computation.40 | loop fusion | flops 3932160 | bytes 6297600 | tf_op jit(solution)/shard_map/convert_element_type | solution.py:181
  320.5 3.1 copy.89
  324.4 1.4 copy.91
  (138 shorter events, 18.9 us)
Async XLA Ops:
  7.2 26.7 %copy-start = (bf16[768,768]{1,0:T(8,128)(2,1)S(1)}, bf16[768,768]{1,0:T(8,128)(2,1)}, u32[]{:S(2)}) copy-start(bf16[768,768]{1,0:T(8,128)(2,1)} %param.39) | copy-start | bytes 3538948
  7.2 4.0 %copy-start.1 = (bf16[1024,768]{1,0:T(8,128)(2,1)S(1)}, bf16[1024,768]{1,0:T(8,128)(2,1)}, u32[]{:S(2)}) copy-start(bf16[1024,768]{1,0:T(8,128)(2,1)} %param.28) | copy-start | bytes 4718596
  7.2 4.0 %copy-start.13 = (f32[768]{0:T(1024)S(1)}, f32[768]{0:T(1024)}, u32[]{:S(2)}) copy-start(f32[768]{0:T(1024)} %param.31) | copy-start | bytes 9220
  7.2 4.0 %copy-start.28 = (f32[768]{0:T(1024)S(1)}, f32[768]{0:T(1024)}, u32[]{:S(2)}) copy-start(f32[768]{0:T(1024)} %param.32) | copy-start | bytes 9220
  7.2 4.0 %copy-start.26 = (f32[576]{0:T(1024)S(1)}, f32[576]{0:T(1024)}, u32[]{:S(2)}) copy-start(f32[576]{0:T(1024)} %param.34) | copy-start | bytes 6916
  7.2 175.7 %all-reduce.10.cloned.1.call-start = ((), (), s32[]{:S(2)}) async-start(), calls=%async_computation.1 | async-start | bytes 12582912 | tf_op jit(solution)/shard_map/psum | solution.py:180
  7.3 3.9 %copy-start.25 = (bf16[768,576]{0,1:T(8,128)(2,1)S(1)}, bf16[768,576]{0,1:T(8,128)(2,1)}, u32[]{:S(2)}) copy-start(bf16[768,576]{0,1:T(8,128)(2,1)} %param.33) | copy-start | bytes 2654212
  34.2 6.8 %copy-start.8 = (bf16[1024,3,3,64]{0,3,2,1:T(8,128)(2,1)}, bf16[1024,3,3,64]{0,3,2,1:T(8,128)(2,1)S(1)}, u32[]{:S(2)}) copy-start(bf16[1024,3,3,64]{0,3,2,1:T(8,128)(2,1)S(1)} %copy.64) | copy-start | bytes 3538948
  34.2 2.0 copy-start.24
  36.2 8.7 %copy-start.32 = (bf16[1024,768]{1,0:T(8,128)(2,1)}, bf16[1024,768]{1,0:T(8,128)(2,1)S(1)}, u32[]{:S(2)}) copy-start(bf16[1024,768]{1,0:T(8,128)(2,1)S(1)} %get-tuple-element.127) | copy-start | bytes 4718596
  51.7 268.2 %all-reduce.8.cloned.1.call-start = ((), (), s32[]{:S(2)}) async-start(), calls=%async_computation | async-start | bytes 14155776 | tf_op jit(solution)/shard_map/psum | solution.py:231
  54.6 4.8 %copy-start.9 = (bf16[1024,3,3,64]{0,3,2,1:T(8,128)(2,1)S(1)}, bf16[1024,3,3,64]{0,3,2,1:T(8,128)(2,1)}, u32[]{:S(2)}) copy-start(bf16[1024,3,3,64]{0,3,2,1:T(8,128)(2,1)} %copy-done.8) | copy-start | bytes 3538948
  54.6 4.8 %copy-start.29 = (f32[768]{0:T(1024)S(1)}, f32[768]{0:T(1024)}, u32[]{:S(2)}) copy-start(f32[768]{0:T(1024)} %param.32) | copy-start | bytes 9220
  59.4 2.6 copy-start.31
  59.4 2.6 copy-start.34
  65.2 1.7 copy-start.19
  65.2 1.8 copy-start.18
  182.9 4.2 %copy-start.17 = (f32[768]{0:T(1024)S(1)}, f32[768]{0:T(1024)}, u32[]{:S(2)}) copy-start(f32[768]{0:T(1024)} %get-tuple-element.135) | copy-start | bytes 9220
  182.9 133.4 %copy-start.15 = (f32[768]{0:T(1024)S(1)}, f32[768]{0:T(1024)}, u32[]{:S(2)}) copy-start(f32[768]{0:T(1024)} %param.42) | copy-start | bytes 9220
  182.9 133.4 %copy-start.16 = (f32[768]{0:T(1024)S(1)}, f32[768]{0:T(1024)}, u32[]{:S(2)}) copy-start(f32[768]{0:T(1024)} %param.36) | copy-start | bytes 9220
  316.3 3.5 %copy-start.23 = (f32[768]{0:T(1024)}, f32[768]{0:T(1024)S(1)}, u32[]{:S(2)}) copy-start(f32[768]{0:T(1024)S(1)} %get-tuple-element.176) | copy-start | bytes 9220
  319.9 3.7 %copy-start.10 = (f32[192,768]{1,0:T(8,128)S(1)}, f32[192,768]{1,0:T(8,128)}, u32[]{:S(2)}) copy-start(f32[192,768]{1,0:T(8,128)} %get-tuple-element.175) | copy-start | bytes 1769476
  319.9 4.5 %copy-start.7 = (f32[768,768]{1,0:T(8,128)S(1)}, f32[768,768]{1,0:T(8,128)}, u32[]{:S(2)}) copy-start(f32[768,768]{1,0:T(8,128)} %get-tuple-element.179) | copy-start | bytes 7077892
  323.6 2.2 copy-start.6
  (13 other events, 15.2 us)
Sparse Core Ops, SparseCore 0:
  51.8 131.0 all-reduce.9
  187.9 118.3 all-reduce.7
where the time goes:
time: 334 us
  blocking collectives  201 us (60%)
  matrix products  43.8 us (13%)
  waiting for transfers between devices  43.6 us (13%)
  other arithmetic  20.4 us (6%)
  between operations  14.7 us (4%)
  local copies, waits for them, and re-layouts  10.5 us (3%)
    psum x1, blocking collectives, on_device(): lax.psum((heads_grad, heads_bias_grad, dense_grad, out_bias_grad, expand_...  129 us
    psum x1, blocking collectives, on_device(): norm_terms = lax.psum(norm_terms, ('dp', 'tensor'))  71.8 us
    psum x1, waiting for transfers between devices, on_device(): branch = lax.psum(branch_part, 'tensor')  43.5 us
    dot_general x12, matrix products, contract(): jnp.einsum(pattern, left_op, right_op, preferred_element_type=jnp.float32)  14.1 us
    unnamed x75, local copies, waits for them, and re-layouts  9.24 us
  transfers between devices with their start and end apart: 2, of which 1 were waited for; matrix products, arithmetic and copies ran while one was open for 7% of the time, Pallas kernels for 0%

commit v1 on v0

--- a/solution.py
+++ b/solution.py
@@ -177,7 +177,7 @@
     branch_part = jnp.dot(context_rows, dense_weight, preferred_element_type=jnp.float32) + jnp.dot(
         activated, shrink_weight, preferred_element_type=jnp.float32
     )
-    branch = lax.psum(branch_part, "tensor")
+    branch = jnp.sum(lax.all_gather(branch_part, "tensor"), axis=0)
     hidden_out = (wide_input + branch + dense_bias + shrink_bias).astype(jnp.bfloat16)
     grad_rows = cotangent.astype(jnp.float32)
     out_bias_grad = jnp.sum(grad_rows, axis=0)

time: 334 us -> 396 us (1.19)
  waiting for transfers between devices: 43.6 us -> 89.2 us
  other arithmetic: 20.4 us -> 28.7 us
  matrix products: 43.8 us -> 51.6 us
  local copies, waits for them, and re-layouts: 10.5 us -> 16.8 us
  blocking collectives: 201 us -> 195 us
    all_gather x0 -> x1, waiting for transfers between devices: none -> 89.1 us  [on_device(): branch = jnp.sum(lax.all_gather(branch_part, 'tensor'), axis=0)]
    psum x1, waiting for transfers between devices: 43.5 us -> 0.01 us  [on_device(): summed_input = lax.psum(input_part, 'tensor')]
    reduce_sum x0 -> x1, other arithmetic: none -> 7.43 us  [on_device(): branch = jnp.sum(lax.all_gather(branch_part, 'tensor'), axis=0)]
    unnamed x75 -> x137, local copies, waits for them, and re-layouts: 9.24 us -> 15.5 us
    dot_general x12, matrix products: 14.1 us -> 18.9 us  [contract(): jnp.einsum(pattern, left_op, right_op, preferred_element_type=jnp.float32)]
  transfers between devices with their start and end apart: 2 -> 3, of which waited for: 1 -> 1; matrix products, arithmetic and copies ran while one was open for 7% -> 11% of each run, Pallas kernels for 0% -> 0%
where the time goes in v1:
time: 396 us
  blocking collectives  195 us (49%)
  waiting for transfers between devices  89.2 us (23%)
  matrix products  51.6 us (13%)
  other arithmetic  28.7 us (7%)
  local copies, waits for them, and re-layouts  16.8 us (4%)
  between operations  14.7 us (4%)
    psum x1, blocking collectives, on_device(): lax.psum((heads_grad, heads_bias_grad, dense_grad, out_bias_grad, expand_...  127 us
    all_gather x1, waiting for transfers between devices, on_device(): branch = jnp.sum(lax.all_gather(branch_part, 'tensor'), axis=0)  89.1 us
    psum x1, blocking collectives, on_device(): norm_terms = lax.psum(norm_terms, ('dp', 'tensor'))  68.2 us
    dot_general x12, matrix products, contract(): jnp.einsum(pattern, left_op, right_op, preferred_element_type=jnp.float32)  18.9 us
    unnamed x137, local copies, waits for them, and re-layouts  15.5 us
  transfers between devices with their start and end apart: 3, of which 1 were waited for; matrix products, arithmetic and copies ran while one was open for 11% of the time, Pallas kernels for 0%

profile of v1, /device:TPU:0, one launch (start us, length us, event | category | flops | bytes accessed | tf_op | source)
XLA Modules:
  0.0 395.9 jit_solution(13312392519725174317)
XLA Ops:
  7.3 1.8 convert_reduce_fusion
  9.2 2.0 fusion.25
  16.2 2.0 fusion
  18.9 2.1 fusion.56
  24.8 3.6 multiply_convert_fusion.2
  29.9 2.3 convolution_add_fusion
  33.8 3.1 multiply_convert_fusion.1
  37.3 5.0 %multiply_convert_fusion = bf16[3,512,1024]{2,1,0:T(8,128)(2,1)S(1)} fusion(f32[3,512,1024]{2,1,0:T(8,128)} %copy-done.6, f32[3,512]{1,0:T(4,128)S(1)} %copy-done.63, f32[3,512]{1,0:T(4,128)S(1)} %log_add_fusion, pred[512,1024]{1,0:T(8,128)(4,1)S(1)} %copy-done.16, bf16[3,1024,64]{1,2,0:T(8,128)(2,1)S(1)} %bitcast.76, f32[1024,3,3,64]{0,3,2,1:T(8,128)} %bitcast.71), kind=kOutput, calls=%fused_computation | convolution fusion | flops 212336640 | bytes 10567680 | tf_op jit(solution)/shard_map/hqd,hkd->hqk/dot_general | solution.py:15
  45.3 2.3 copy-done.2
  48.2 1.9 fusion.52
  50.5 1.9 copy-done.8
  52.8 3.4 fusion.98
  58.0 5.1 %fusion.23 = (f32[768]{0:T(1024)}, f32[1024]{0:T(1024)S(1)}, f32[1024]{0:T(1024)S(1)}, f32[768]{0:T(1024)}, f32[768]{0:T(1024)}, /*index=5*/f32[1024]{0:T(1024)S...) fusion(bf16[1024,768]{1,0:T(8,128)(2,1)S(1)} %copy-done.3, f32[1024]{0:T(1024)S(1)} %add_rsqrt_fusion, ...), kind=kOutput, calls=%fused_computation.34 | convolution fusion | flops 919331840 | bytes 9971712 | tf_op jit(solution)/shard_map/dot_general | solution.py:207
  64.3 89.1 %all-gather.3.cloned.1.call-done = f32[4096,768]{1,0:T(8,128)} async-done(((f32[1024,768]{1,0:T(8,128)}), f32[4096,768]{1,0:T(8,128)}) %all-gather.3.cloned.1.call-update) | async-done | bytes 12582928 | tf_op jit(solution)/shard_map/all_gather | solution.py:180
  153.5 7.4 %reduce_sum.168 = f32[1024,768]{1,0:T(8,128)} reduce(f32[4,1024,768]{2,1,0:T(8,128)} %bitcast.63, f32[]{:T(128)} %constant.131.clone.1), dimensions={0}, to_apply=%region_6.7 | reduce | flops 2359296 | bytes 15728644 | tf_op jit(solution)/shard_map/reduce_sum | solution.py:180
  160.9 6.2 %fusion.20 = (f32[1024,768]{1,0:T(8,128)}, bf16[1024,768]{1,0:T(8,128)(2,1)}) fusion(bf16[1024,768]{1,0:T(8,128)(2,1)S(1)} %copy-done.3, f32[1024,768]{1,0:T(8,128)} %copy-done.10, f32[1024,768]{1,0:T(8,128)} %get-tuple-element.132, f32[1024]{0:T(1024)S(1)} %broadcast_multiply_fusion.1, f32[1024]{0:T(1024)S(1)} %broadcast_multiply_fusion.2, ...), kind=kLoop, calls=%fused_computation.31 | loop fusion | flops 13369344 | bytes 15765504 | tf_op jit(solution)/shard_map/add | solution.py:209
  167.1 2.8 fusion.102
  170.0 4.8 %fusion.103 = f32[768,768]{1,0:T(8,128)} fusion(bf16[1024,768]{1,0:T(8,128)(2,1)} %copy-done.59, bf16[1024,768]{1,0:T(8,128)(2,1)} %param.43), kind=kOutput, calls=%fused_computation.159 | convolution fusion | flops 1207959552 | bytes 5505024 | tf_op jit(solution)/shard_map/dot_general | solution.py:184
  174.8 2.6 fusion.92
  177.4 3.2 fusion.58
  182.3 68.2 %psum.64 = f32[4,768]{1,0:T(4,128)S(1)} all-reduce(f32[4,768]{1,0:T(4,128)S(1)} %pad_maximum_fusion.3), channel_id=1, replica_groups=mesh['dp'=32,'tensor'=4] {'dp','tensor'}, use_global_device_ids=true, to_apply=%region_18.19 | all-reduce | flops 3072 | bytes 24576 | tf_op jit(solution)/shard_map/psum | solution.py:220
  251.2 4.2 %convert_reduce_fusion.1 = (f32[768]{0:T(1024)S(1)}, bf16[1024,768]{1,0:T(8,128)(2,1)}) fusion(bf16[1024,768]{1,0:T(8,128)(2,1)} %param.43, f32[1024,768]{1,0:T(8,128)} %all-reduce.7.cloned.1.call-done), kind=kLoop, calls=%fused_computation.11 | loop fusion | flops 3144960 | bytes 6294528 | tf_op jit(solution)/shard_map/reduce_sum | solution.py:183
  255.4 126.7 %all-reduce.2 = (f32[576]{0:T(1024)}, f32[768]{0:T(1024)S(1)}, f32[768]{0:T(1024)}) all-reduce(f32[576]{0:T(1024)S(1)} %reduce_sum.180, f32[768]{0:T(1024)S(1)} %get-tuple-element.105, f32[768]{0:T(1024)S(1)} %copy-done.41), channel_id=1, replica_groups=mesh['dp'=32,'tensor'=4] {'dp'}, use_global_device_ids=true, to_apply=%region_21.22 | all-reduce | flops 2112 | bytes 16896 | tf_op jit(solution)/shard_map/psum | solution.py:231
  382.7 3.1 copy.88
  (204 shorter events, 26.4 us)
Async XLA Ops:
  7.2 17.6 %copy-start = (bf16[768,768]{1,0:T(8,128)(2,1)S(1)}, bf16[768,768]{1,0:T(8,128)(2,1)}, u32[]{:S(2)}) copy-start(bf16[768,768]{1,0:T(8,128)(2,1)} %param.39) | copy-start | bytes 3538948
  7.2 4.0 %copy-start.3 = (bf16[1024,768]{1,0:T(8,128)(2,1)S(1)}, bf16[1024,768]{1,0:T(8,128)(2,1)}, u32[]{:S(2)}) copy-start(bf16[1024,768]{1,0:T(8,128)(2,1)} %param.28) | copy-start | bytes 4718596
  7.2 4.0 %copy-start.35 = (f32[768]{0:T(1024)S(1)}, f32[768]{0:T(1024)}, u32[]{:S(2)}) copy-start(f32[768]{0:T(1024)} %param.31) | copy-start | bytes 9220
  7.2 4.0 %copy-start.55 = (f32[768]{0:T(1024)S(1)}, f32[768]{0:T(1024)}, u32[]{:S(2)}) copy-start(f32[768]{0:T(1024)} %param.32) | copy-start | bytes 9220
  7.2 4.0 %copy-start.52 = (f32[576]{0:T(1024)S(1)}, f32[576]{0:T(1024)}, u32[]{:S(2)}) copy-start(f32[576]{0:T(1024)} %param.34) | copy-start | bytes 6916
  7.2 146.2 %all-gather.3.cloned.1.call-start = ((), (), s32[]{:S(2)}) async-start(), calls=%async_computation.1 | async-start | bytes 15728640 | tf_op jit(solution)/shard_map/all_gather | solution.py:180
  12.6 5.7 %copy-start.17 = (f32[1024,576]{0,1:T(8,128)}, f32[1024,576]{0,1:T(8,128)S(1)}, u32[]{:S(2)}) copy-start(f32[1024,576]{0,1:T(8,128)S(1)} %convolution_add_fusion.1) | copy-start | bytes 7077892
  13.4 10.0 %copy-start.20 = (bf16[3,1024,64]{1,2,0:T(8,128)(2,1)}, bf16[3,1024,64]{1,2,0:T(8,128)(2,1)S(1)}, u32[]{:S(2)}) copy-start(bf16[3,1024,64]{1,2,0:T(8,128)(2,1)S(1)} %fusion.62) | copy-start | bytes 1179652
  14.9 6.4 %copy-start.21 = (bf16[3,1024,64]{1,2,0:T(8,128)(2,1)}, bf16[3,1024,64]{1,2,0:T(8,128)(2,1)S(1)}, u32[]{:S(2)}) copy-start(bf16[3,1024,64]{1,2,0:T(8,128)(2,1)S(1)} %maximum_bitcast_fusion.4) | copy-start | bytes 1179652
  24.8 5.1 %copy-start.9 = (bf16[3,1024,64]{1,2,0:T(8,128)(2,1)}, bf16[3,1024,64]{1,2,0:T(8,128)(2,1)S(1)}, u32[]{:S(2)}) copy-start(bf16[3,1024,64]{1,2,0:T(8,128)(2,1)S(1)} %pad_maximum_fusion.1) | copy-start | bytes 1179652
  32.2 219.0 %all-reduce.7.cloned.1.call-start = ((), (), s32[]{:S(2)}) async-start(), calls=%async_computation | async-start | bytes 6291456 | tf_op jit(solution)/shard_map/psum | solution.py:221
  32.3 4.6 %copy-start.22 = (bf16[3,1024,64]{1,2,0:T(8,128)(2,1)S(1)}, bf16[3,1024,64]{1,2,0:T(8,128)(2,1)}, u32[]{:S(2)}) copy-start(bf16[3,1024,64]{1,2,0:T(8,128)(2,1)} %copy-done.21) | copy-start | bytes 1179652
  42.3 5.9 %slice-start = ((s8[6291456]{0:T(1024)(128)(4,1)}), s8[4194304]{0:T(1024)(128)(4,1)S(1)}, s32[]{:S(2)}) async-start(s8[6291456]{0:T(1024)(128)(4,1)} %bitcast.64), calls=%async_computation.3 | async-start | bytes 8388608
  44.2 4.0 %slice-start.1 = ((s8[6291456]{0:T(1024)(128)(4,1)}), s8[2097152]{0:T(1024)(128)(4,1)S(1)}, s32[]{:S(2)}) async-start(s8[6291456]{0:T(1024)(128)(4,1)} %bitcast.64), calls=%async_computation.4 | async-start | bytes 4194304
  50.1 6.1 %copy-start.11 = (f32[1024,3,1,64]{0,3,1,2:T(8,128)}, f32[1024,3,1,64]{0,3,1,2:T(8,128)S(1)}, u32[]{:S(2)}) copy-start(f32[1024,3,1,64]{0,3,1,2:T(8,128)S(1)} %fusion.52) | copy-start | bytes 2359300
  50.5 7.2 %copy-start.18 = (bf16[1024,3,3,64]{0,3,2,1:T(8,128)(2,1)}, bf16[1024,3,3,64]{0,3,2,1:T(8,128)(2,1)S(1)}, u32[]{:S(2)}) copy-start(bf16[1024,3,3,64]{0,3,2,1:T(8,128)(2,1)S(1)} %copy.64) | copy-start | bytes 3538948
  57.7 5.4 %copy-start.10 = (f32[1024,768]{1,0:T(8,128)}, f32[1024,768]{1,0:T(8,128)S(1)}, u32[]{:S(2)}) copy-start(f32[1024,768]{1,0:T(8,128)S(1)} %fusion.60) | copy-start | bytes 9437188
  167.1 215.0 %all-reduce.9.cloned.1.call-start = ((), (), s32[]{:S(2)}) async-start(), calls=%async_computation.2 | async-start | bytes 14155776 | tf_op jit(solution)/shard_map/psum | solution.py:231
  169.9 4.8 %copy-start.19 = (bf16[1024,3,3,64]{0,3,2,1:T(8,128)(2,1)S(1)}, bf16[1024,3,3,64]{0,3,2,1:T(8,128)(2,1)}, u32[]{:S(2)}) copy-start(bf16[1024,3,3,64]{0,3,2,1:T(8,128)(2,1)} %copy-done.18) | copy-start | bytes 3538948
  169.9 4.8 %copy-start.37 = (f32[768]{0:T(1024)S(1)}, f32[768]{0:T(1024)}, u32[]{:S(2)}) copy-start(f32[768]{0:T(1024)} %param.31) | copy-start | bytes 9220
  170.0 4.8 %copy-start.56 = (f32[768]{0:T(1024)S(1)}, f32[768]{0:T(1024)}, u32[]{:S(2)}) copy-start(f32[768]{0:T(1024)} %param.32) | copy-start | bytes 9220
  251.2 4.2 %copy-start.41 = (f32[768]{0:T(1024)S(1)}, f32[768]{0:T(1024)}, u32[]{:S(2)}) copy-start(f32[768]{0:T(1024)} %get-tuple-element.135) | copy-start | bytes 9220
  382.1 5.9 %copy-start.47 = (f32[768]{0:T(1024)}, f32[768]{0:T(1024)S(1)}, u32[]{:S(2)}) copy-start(f32[768]{0:T(1024)S(1)} %get-tuple-element.176) | copy-start | bytes 9220
  382.1 4.5 %copy-start.14 = (f32[768,768]{1,0:T(8,128)S(1)}, f32[768,768]{1,0:T(8,128)}, u32[]{:S(2)}) copy-start(f32[768,768]{1,0:T(8,128)} %get-tuple-element.179) | copy-start | bytes 7077892
  (45 other events, 92.2 us)
Sparse Core Ops, SparseCore 0:
  32.3 121.0 all-gather.2
  167.2 78.0 all-reduce.6
  250.3 118.1 all-reduce.8
